TPU v7x, 32 devices: a whole 2x2x4 slice. The times are simulated.
32 devices in a mesh: fsdp: 4 (over x, core), context: 4 (over z), tensor: 2 (over y).
Axes of the slice: x: 2, y: 2, z: 4, core: 2. Of those that a mesh axis runs over, the one named last changes fastest.
Arguments:
- block_input: float32 [8192, 768], P(('fsdp', 'context')), may hold values from -18 to 18
- ln1_gain: float32 [768], replicated, may hold values from 0.1 to 1.9
- ln1_shift: float32 [768], replicated, may hold values from -3 to 3
- qkv_weight: float32 [768, 3, 768], P(('fsdp', 'context'), None, 'tensor'), may hold values from -0.21875 to 0.21875
- qkv_bias: float32 [3, 768], P(None, 'tensor'), may hold values from -3 to 3
- feat_query: float32 [12, 64, 64], P('tensor'), may hold values from -1.5 to 1.5
- feat_key: float32 [12, 64, 64], P('tensor'), may hold values from -1.5 to 1.5
- out_weight: float32 [768, 768], P('tensor', ('fsdp', 'context')), may hold values from -3.5 to 3.5
- out_bias: float32 [768], replicated, may hold values from -3 to 3
- ln2_gain: float32 [768], replicated, may hold values from 0.1 to 1.9
- ln2_shift: float32 [768], replicated, may hold values from -3 to 3
- up_weight: float32 [768, 3072], P(('fsdp', 'context'), 'tensor'), may hold values from -0.21875 to 0.21875
- up_bias: float32 [3072], P('tensor'), may hold values from -3 to 3
- down_weight: float32 [3072, 768], P('tensor', ('fsdp', 'context')), may hold values from -0.109375 to 0.109375
- down_bias: float32 [768], replicated, may hold values from -3 to 3
- lengths: int32 [4], replicated, may hold values from 1024 to 2048, as said below
- deal: int32 [128], P(('fsdp', 'context')), may hold values from 0 to 127, as said below
- cotangent: float32 [8192, 768], P(('fsdp', 'context')), may hold values from -6 to 6
Outputs:
- dealt_output: float32 [128, 64, 768], P(('fsdp', 'context'), 'tensor')
- rms: float32 [3], replicated
- grad_input: float32 [8192, 768], P(('fsdp', 'context'))
- grad_ln1_gain: float32 [768], replicated
- grad_ln1_shift: float32 [768], replicated
- grad_qkv_weight: float32 [768, 3, 768], P(('fsdp', 'context'), None, 'tensor')
- grad_qkv_bias: float32 [3, 768], P(None, 'tensor')
- grad_feat_query: float32 [12, 64, 64], P('tensor')
- grad_feat_key: float32 [12, 64, 64], P('tensor')
- grad_out_weight: float32 [768, 768], P('tensor', ('fsdp', 'context'))
- grad_out_bias: float32 [768], replicated
- grad_ln2_gain: float32 [768], replicated
- grad_ln2_shift: float32 [768], replicated
- grad_up_weight: float32 [768, 3072], P(('fsdp', 'context'), 'tensor')
- grad_up_bias: float32 [3072], P('tensor')
- grad_down_weight: float32 [3072, 768], P('tensor', ('fsdp', 'context'))
- grad_down_bias: float32 [768], replicated
Inputs may be any that keep to these rules, and one draw needn't show every extreme that they name: Sequence lengths; the 4 lengths sum to exactly 8160, and the last of them is exactly 2048. deal is a permutation of the 128 groups. Group j of the device with fsdp index f and context index e (groups numbered along fsdp, then context, then position) goes to position (f * 4 + d) * 8 + e * 2 + r, where the 8 groups of one device take every pair of d < 4 and r < 2 once.
All inputs are finite; a program needn't handle non-finite values.
Results may differ from a plain program's by a relative error of at most 0.0003.
Values sent between devices are 32-bit elements; how exact they have to be, the bound alone decides.
No kernel may reach another device: no remote copies, remote signals or barrier semaphores. Data moves between devices by JAX's collectives and lax.ppermute only.
A program may use at most 128 MiB of HBM per device.

v0:
```python
from functools import partial
import jax
import jax.numpy as jnp
from jax import lax
from jax.sharding import PartitionSpec as P

HIGH = lax.Precision.HIGHEST
NORM_EPS = 1e-05


def entering(x, axis, combine, identity, reverse):
    count, place = (lax.axis_size(axis), lax.axis_index(axis))
    everything = jax.tree.map(lambda part: lax.all_gather(part, axis), x)
    start = jax.tree.map(
        lambda part, zero: jnp.broadcast_to(jnp.asarray(zero, part.dtype), part.shape), x, identity
    )

    def lap(k, before):
        at = count - 1 - k if reverse else k
        reached = at > place if reverse else at < place
        new = combine(before, jax.tree.map(lambda part: part[at], everything))
        return jax.tree.map(lambda a, b: jnp.where(reached, a, b), new, before)

    return lax.fori_loop(0, count, lap, start)


def layer_norm(values, gain, shift):
    middle = jnp.mean(values, axis=-1, keepdims=True)
    centred = values - middle
    spread = jnp.mean(centred * centred, axis=-1, keepdims=True)
    return centred * lax.rsqrt(spread + NORM_EPS) * gain + shift


def feature_map(heads, weight):
    logits = jnp.einsum("rhd,hde->rhe", heads, weight, precision=HIGH)
    return jnp.concatenate(
        [jax.nn.softmax(logits, axis=-1), jax.nn.softmax(-logits, axis=-1)], axis=-1
    )


def segment_of(places, ends, total, number):
    found = jnp.sum((ends[None, :] <= places[:, None]).astype(jnp.int32), axis=1)
    found = jnp.where(places < 0, -1, found)
    return jnp.where(places >= total, number + 1, found)


def project(normed, weight, bias):
    return jnp.einsum("rd,dke->rke", normed, weight, precision=HIGH) + bias


def mlp_part(normed, up_full, up_bias, down_full):
    active = jax.nn.gelu(jnp.dot(normed, up_full, precision=HIGH) + up_bias, approximate=True)
    return jnp.dot(active, down_full, precision=HIGH)


def chain_join(earlier, later):
    passing = 1.0 - later[2]
    return (
        later[0] + passing * earlier[0],
        later[1] + passing * earlier[1],
        jnp.maximum(earlier[2], later[2]),
    )


def local_part(queries, keys, values, weight_q, weight_k, segment, seg_first, block):
    phi_q = feature_map(queries, weight_q)
    phi_k = feature_map(keys, weight_k)
    count_rows, local_heads, head_dim = values.shape
    feats = phi_q.shape[2]
    blocks = count_rows // block
    lower = jnp.arange(block)[:, None] >= jnp.arange(block)[None, :]

    def block_step(carry, pieces):
        state, normer, seg_carry = carry
        piece_q, piece_k, piece_v, seg_piece = pieces
        allowed = jnp.logical_and(lower, seg_piece[:, None] == seg_piece[None, :]).astype(
            jnp.float32
        )
        scores = jnp.einsum("ihf,jhf->hij", piece_q, piece_k, precision=HIGH) * allowed[None]
        numer = jnp.einsum("hij,jhd->ihd", scores, piece_v, precision=HIGH)
        denom = jnp.einsum("hij->ih", scores)
        carried = (seg_piece == seg_carry).astype(jnp.float32)
        numer = numer + carried[:, None, None] * jnp.einsum(
            "ihf,hfd->ihd", piece_q, state, precision=HIGH
        )
        denom = denom + carried[:, None] * jnp.einsum("ihf,hf->ih", piece_q, normer, precision=HIGH)
        final_seg = seg_piece[-1]
        stays = (final_seg == seg_carry).astype(jnp.float32)
        tail_k = piece_k * (seg_piece == final_seg).astype(jnp.float32)[:, None, None]
        state = stays * state + jnp.einsum("jhf,jhd->hfd", tail_k, piece_v, precision=HIGH)
        normer = stays * normer + jnp.sum(tail_k, axis=0)
        return ((state, normer, final_seg), (numer, denom))

    def blocked(array):
        return array.reshape((blocks, block) + array.shape[1:])

    start = (
        jnp.zeros((local_heads, feats, head_dim), jnp.float32),
        jnp.zeros((local_heads, feats), jnp.float32),
        seg_first,
    )
    (state, normer, _), (numer, denom) = lax.scan(
        jax.checkpoint(block_step),
        start,
        (blocked(phi_q), blocked(phi_k), blocked(values), blocked(segment)),
    )
    return (
        phi_q,
        numer.reshape(count_rows, local_heads, head_dim),
        denom.reshape(count_rows, local_heads),
        state,
        normer,
    )


def body(
    block_input,
    ln1_gain,
    ln1_shift,
    qkv_weight,
    qkv_bias,
    feat_query,
    feat_key,
    out_weight,
    out_bias,
    ln2_gain,
    ln2_shift,
    up_weight,
    up_bias,
    down_weight,
    down_bias,
    lengths,
    deal,
    cotangent,
):
    count_rows, width = block_input.shape
    local_heads, head_dim = (feat_query.shape[0], feat_query.shape[1])
    local_width = local_heads * head_dim
    offset = lax.axis_index(("fsdp", "context")) * count_rows
    total = count_rows * lax.axis_size(("fsdp", "context"))
    ends = jnp.cumsum(lengths)
    used = ends[-1]
    number = lengths.shape[0]
    places = offset + jnp.arange(count_rows, dtype=jnp.int32)
    segment = segment_of(places, ends, total, number)
    edges = segment_of(offset + jnp.array([-1, count_rows], dtype=jnp.int32), ends, total, number)
    seg_first = segment[0]
    seg_final = segment[-1]
    carry_in = (edges[0] == seg_first).astype(jnp.float32)
    breaks = (edges[0] != seg_final).astype(jnp.float32)
    valid = (places < used).astype(jnp.float32)[:, None]
    block = min(512, count_rows)
    qkv_full, out_full, up_full, down_full = (
        lax.all_gather(qkv_weight, ("fsdp", "context"), axis=0, tiled=True),
        lax.all_gather(out_weight, ("fsdp", "context"), axis=1, tiled=True),
        lax.all_gather(up_weight, ("fsdp", "context"), axis=0, tiled=True),
        lax.all_gather(down_weight, ("fsdp", "context"), axis=1, tiled=True),
    )
    normed1 = layer_norm(block_input, ln1_gain, ln1_shift)
    qkv = project(normed1, qkv_full, qkv_bias)
    queries = qkv[:, 0, :].reshape(count_rows, local_heads, head_dim)
    keys = qkv[:, 1, :].reshape(count_rows, local_heads, head_dim)
    values = qkv[:, 2, :].reshape(count_rows, local_heads, head_dim)
    attend_local = partial(local_part, segment=segment, seg_first=seg_first, block=block)
    phi_q, numer_local, denom_local, state_tail, norm_tail = attend_local(
        queries, keys, values, feat_query, feat_key
    )
    identity = (jnp.zeros_like(state_tail), jnp.zeros_like(norm_tail), jnp.zeros((), jnp.float32))
    state_scan, norm_scan, _ = entering(
        (state_tail, norm_tail, breaks), ("fsdp", "context"), chain_join, identity, False
    )
    state_in = carry_in * state_scan
    norm_in = carry_in * norm_scan
    first_rows = (segment == seg_first).astype(jnp.float32)[:, None, None]
    masked_q = phi_q * first_rows
    numer = numer_local + jnp.einsum("rhf,hfd->rhd", masked_q, state_in, precision=HIGH)
    denom = denom_local + jnp.einsum("rhf,hf->rh", masked_q, norm_in, precision=HIGH)
    attended = numer / denom[:, :, None]
    attended_flat = attended.reshape(count_rows, local_width)
    attn_part = jnp.dot(attended_flat, out_full, precision=HIGH)
    attn = lax.psum(attn_part, "tensor") + out_bias
    hidden = block_input + attn
    normed2 = layer_norm(hidden, ln2_gain, ln2_shift)
    slots = deal.shape[0]
    group_rows = count_rows // slots
    part_rows = group_rows // lax.axis_size("tensor")
    part_start = lax.axis_index("tensor") * part_rows
    per_peer = slots // lax.axis_size("context")
    slot_of = deal // slots % lax.axis_size("context") * per_peer + deal % per_peer
    counting = jnp.arange(slots, dtype=jnp.int32)
    source_of = jnp.sum(
        jnp.where(slot_of[None, :] == counting[:, None], counting[None, :], 0), axis=1
    )
    mlp_terms = mlp_part(normed2, up_full, up_bias, down_full)
    mlp = lax.psum(mlp_terms, "tensor") + down_bias
    result = hidden + mlp
    outbound = jnp.take(result.reshape(slots, group_rows, width), source_of, axis=0)
    dealt_whole = lax.all_to_all(outbound, "context", split_axis=0, concat_axis=0, tiled=True)
    dealt_output = lax.dynamic_slice_in_dim(dealt_whole, part_start, part_rows, 1)
    squares = jnp.stack(
        [jnp.sum(valid * result * result), jnp.sum(valid * attn * attn), jnp.sum(valid * mlp * mlp)]
    )
    inbound = lax.all_to_all(
        cotangent.reshape(slots, group_rows, width),
        "context",
        split_axis=0,
        concat_axis=0,
        tiled=True,
    )
    grad_y = jnp.take(inbound, slot_of, axis=0).reshape(count_rows, width) * valid
    grad_down_bias = jnp.sum(grad_y, axis=0)
    _, mlp_backward = jax.vjp(mlp_part, normed2, up_full, up_bias, down_full)
    grad_normed2_part, grad_up_full, grad_up_bias, grad_down_full = mlp_backward(grad_y)
    grad_normed2 = lax.psum(grad_normed2_part, "tensor")
    _, norm2_backward = jax.vjp(layer_norm, hidden, ln2_gain, ln2_shift)
    grad_hidden_norm, grad_ln2_gain, grad_ln2_shift = norm2_backward(grad_normed2)
    grad_hidden = grad_y + grad_hidden_norm
    grad_out_bias = jnp.sum(grad_hidden, axis=0)
    grad_out_full = jnp.einsum("rd,re->de", attended_flat, grad_hidden, precision=HIGH)
    grad_attended = jnp.einsum("re,de->rd", grad_hidden, out_full, precision=HIGH).reshape(
        count_rows, local_heads, head_dim
    )
    grad_numer = grad_attended / denom[:, :, None]
    grad_denom = -jnp.sum(grad_attended * attended, axis=2) / denom
    grad_state_in = carry_in * jnp.einsum("rhf,rhd->hfd", masked_q, grad_numer, precision=HIGH)
    grad_norm_in = carry_in * jnp.einsum("rhf,rh->hf", masked_q, grad_denom, precision=HIGH)
    grad_phi_extra = first_rows * (
        jnp.einsum("rhd,hfd->rhf", grad_numer, state_in, precision=HIGH)
        + grad_denom[:, :, None] * norm_in[None, :, :]
    )
    grad_state_tail, grad_norm_tail, _ = entering(
        (grad_state_in, grad_norm_in, breaks), ("fsdp", "context"), chain_join, identity, True
    )
    _, attention_backward = jax.vjp(attend_local, queries, keys, values, feat_query, feat_key)
    grad_queries, grad_keys, grad_values, grad_feat_query, grad_feat_key = attention_backward(
        (grad_phi_extra, grad_numer, grad_denom, grad_state_tail, grad_norm_tail)
    )
    grad_qkv = jnp.stack(
        [
            grad_queries.reshape(count_rows, local_width),
            grad_keys.reshape(count_rows, local_width),
            grad_values.reshape(count_rows, local_width),
        ],
        axis=1,
    )
    _, project_backward = jax.vjp(project, normed1, qkv_full, qkv_bias)
    grad_normed1_part, grad_qkv_full, grad_qkv_bias = project_backward(grad_qkv)
    grad_normed1 = lax.psum(grad_normed1_part, "tensor")
    _, norm1_backward = jax.vjp(layer_norm, block_input, ln1_gain, ln1_shift)
    grad_input_norm, grad_ln1_gain, grad_ln1_shift = norm1_backward(grad_normed1)
    grad_input = grad_hidden + grad_input_norm
    grad_qkv_weight, grad_out_weight, grad_up_weight, grad_down_weight = (
        lax.psum_scatter(grad_qkv_full, ("fsdp", "context"), scatter_dimension=0, tiled=True),
        lax.psum_scatter(grad_out_full, ("fsdp", "context"), scatter_dimension=1, tiled=True),
        lax.psum_scatter(grad_up_full, ("fsdp", "context"), scatter_dimension=0, tiled=True),
        lax.psum_scatter(grad_down_full, ("fsdp", "context"), scatter_dimension=1, tiled=True),
    )
    summed = lax.psum(
        (
            grad_ln1_gain,
            grad_ln1_shift,
            grad_qkv_bias,
            grad_feat_query,
            grad_feat_key,
            grad_out_bias,
            grad_ln2_gain,
            grad_ln2_shift,
            grad_up_bias,
            grad_down_bias,
            squares,
        ),
        ("fsdp", "context"),
    )
    rms = jnp.sqrt(summed[10] / (used.astype(jnp.float32) * width))
    return (
        dealt_output,
        rms,
        grad_input,
        summed[0],
        summed[1],
        grad_qkv_weight,
        summed[2],
        summed[3],
        summed[4],
        grad_out_weight,
        summed[5],
        summed[6],
        summed[7],
        grad_up_weight,
        summed[8],
        grad_down_weight,
        summed[9],
    )


def solution(mesh):
    in_specs = (
        P(("fsdp", "context"), None),
        P(),
        P(),
        P(("fsdp", "context"), None, "tensor"),
        P(None, "tensor"),
        P("tensor", None, None),
        P("tensor", None, None),
        P("tensor", ("fsdp", "context")),
        P(),
        P(),
        P(),
        P(("fsdp", "context"), "tensor"),
        P("tensor"),
        P("tensor", ("fsdp", "context")),
        P(),
        P(),
        P(("fsdp", "context")),
        P(("fsdp", "context"), None),
    )
    out_specs = (
        P(("fsdp", "context"), "tensor", None),
        P(),
        P(("fsdp", "context"), None),
        P(),
        P(),
        P(("fsdp", "context"), None, "tensor"),
        P(None, "tensor"),
        P("tensor", None, None),
        P("tensor", None, None),
        P("tensor", ("fsdp", "context")),
        P(),
        P(),
        P(),
        P(("fsdp", "context"), "tensor"),
        P("tensor"),
        P("tensor", ("fsdp", "context")),
        P(),
    )
    return jax.shard_map(body, mesh=mesh, in_specs=in_specs, out_specs=out_specs, check_vma=False)
```

profile of v0, /device:TPU:0, one launch (start us, length us, event | category | flops | bytes accessed | tf_op | source)
XLA Modules:
  0.0 1227.2 jit_solution(8723379923862665840)
XLA Ops:
  13.2 47.0 %all-gather.13.cloned.1.call-done = f32[768,3,384]{2,0,1:T(8,128)} async-done(((f32[48,3,384]{2,0,1:T(8,128)}), f32[768,3,384]{2,0,1:T(8,128)}) %all-gather.13.cloned.1.call-update) | async-done | bytes 3538960 | tf_op jit(solution)/shard_map/all_gather | solution.py:154
  60.3 8.5 convolution_add_fusion.1
  74.2 2.6 fusion.35
  82.2 43.4 %all-reduce = f32[16]{0:T(128)} all-reduce(f32[16]{0:T(128)S(1)} %dynamic-update-slice), channel_id=1, replica_groups=mesh['fsdp'=4,'context'=4,'tensor'=2] {'fsdp','context'}, use_global_device_ids=true, to_apply=%add | all-reduce | flops 16 | bytes 128
  130.5 31.8 %all-gather.4 = f32[16,6,128]{2,1,0:T(8,128)} all-gather(f32[1,6,128]{2,1,0:T(8,128)S(1)} %bitcast.196), channel_id=3, replica_groups=mesh['fsdp'=4,'context'=4,'tensor'=2] {'fsdp','context'}, dimensions={0}, use_global_device_ids=true | all-gather | bytes 52224 | tf_op jit(solution)/shard_map/all_gather | solution.py:13
  165.9 8.0 multiply_reduce_fusion
  174.0 111.7 %while.22 = (s32[]{:T(128)}, f32[6,128,64]{2,1,0:T(8,128)}, f32[6,128]{1,0:T(8,128)}, s32[]{:T(128)}, f32[16,6,128,64]{2,3,1,0:T(8,128)}, /*index=5*/f32[16]{0:T...) while((s32[]{:T(128)}, f32[6,128,64]{2,1,0:T(8,128)}, f32[6,128]{1,0:T(8,128)}, ...), condition=%wide.region_15.16_spmd.clone, body=%wide.region_14.15_spmd.clone.sunk | while | flops 199685 | bytes 1385643 | solution.py:24
  290.9 6.3 fusion.59
  297.2 6.6 fusion.167
  304.4 3.6 all-to-all-start.1
  310.1 33.8 %all-to-all-done.1 = f32[8,64,768]{2,1,0:T(8,128)S(1)} async-done(((f32[8,64,768]{2,1,0:T(8,128)}), f32[8,64,768]{2,1,0:T(8,128)S(1)}, u32[]{:S(2)}, u32[]{:S(2)}) %all-to-all-start.1) | async-done | bytes 1572896 | tf_op jit(solution)/shard_map/all_to_all | solution.py:203
  345.7 2.2 multiply_reduce_fusion.1
  349.3 11.4 fusion.168
  362.8 47.3 %all-gather.17.cloned.1.call-done = f32[768,1536]{1,0:T(8,128)} async-done(((f32[48,1536]{1,0:T(8,128)}), f32[768,1536]{1,0:T(8,128)}) %all-gather.17.cloned.1.call-update) | async-done | bytes 4718608 | tf_op jit(solution)/shard_map/all_gather | solution.py:156
  410.1 14.9 %fusion.155 = (f32[1536]{0:T(1024)}, f32[512,1536]{1,0:T(8,128)S(1)}, f32[512,1536]{1,0:T(8,128)}) fusion(f32[512,1536]{1,0:T(8,128)} %fusion.168, f32[1536]{0:T(1024)S(1)} %copy-done.118, f32[768,1536]{1,0:T(8,128)} %all-gather.17.cloned.1.call-done, f32[512,768]{1,0:T(8,128)S(1)} %get-tuple-element.631, f32[768]{0:T(1024)S(1)} %copy-done.83, ...), kind=kOutput, calls=%fused_computation.257 | convolution fusion | flops 7265843712 | bytes 15751168 | tf_op jit(solution)/shard_map/dot_general | solution.py:52
  426.6 9.0 fusion.169
  435.9 50.0 %all-reduce.11.cloned.1.call-done = f32[512,768]{1,0:T(8,128)} async-done(((f32[512,768]{1,0:T(8,128)}), f32[512,768]{1,0:T(8,128)}) %all-reduce.11.cloned.1.call-update) | async-done | bytes 1572880 | tf_op jit(solution)/shard_map/psum | solution.py:214
  485.9 2.7 multiply_reduce_fusion.2
  495.3 2.6 fusion.71
  498.8 2.9 pad_maximum_fusion.1
  503.5 12.7 %fusion.38 = f32[512,768]{1,0:T(8,128)} fusion(f32[1536,768]{0,1:T(8,128)} %all-gather.19.cloned.1.call-done, f32[512,1536]{1,0:T(8,128)S(1)} %copy-done.124), kind=kOutput, calls=%fused_computation.80 | convolution fusion | flops 7254048768 | bytes 9437184 | tf_op jit(solution)/shard_map/dot_general | solution.py:53
  517.7 35.5 %all-gather.5 = f32[16,6,128]{2,1,0:T(8,128)} all-gather(f32[1,6,128]{2,1,0:T(8,128)S(1)} %fusion.126), channel_id=5, replica_groups=mesh['fsdp'=4,'context'=4,'tensor'=2] {'fsdp','context'}, dimensions={0}, use_global_device_ids=true | all-gather | bytes 52224 | tf_op jit(solution)/shard_map/all_gather | solution.py:13
  553.3 111.7 %while.23 = (s32[]{:T(128)}, f32[6,128,64]{2,1,0:T(8,128)}, f32[6,128]{1,0:T(8,128)}, s32[]{:T(128)}, f32[16,6,128,64]{2,3,1,0:T(8,128)}, /*index=5*/f32[16]{0:T...) while((s32[]{:T(128)}, f32[6,128,64]{2,1,0:T(8,128)}, ...), condition=%wide.region_31.33_spmd.clone, body=%wide.region_30.32_spmd.clone.sunk | while | flops 199689 | bytes 1385705 | solution.py:24
  668.4 2.6 copy.110
  671.0 7.3 fusion.171
  678.4 5.1 fusion.88
  683.6 5.3 fusion.12
  688.9 8.5 fusion.13
  697.4 4.1 fusion.8
  704.8 2.3 copy.118
  707.1 3.3 bitcast_add_fusion.4
  714.2 2.3 copy.117
  716.6 2.7 fusion.90
  725.2 2.3 copy.116
  727.5 10.4 convolution_bitcast_fusion
  738.0 5.4 fusion.172
  743.5 12.1 fusion.62
  755.6 12.1 fusion.37
  767.9 3.0 fusion.83
  772.7 10.1 fusion.30
  783.6 37.0 %all-reduce.15.cloned.1.call-done = (f32[512,768]{1,0:T(8,128)}, f32[512,768]{1,0:T(8,128)}) async-done(((f32[512,768]{1,0:T(8,128)}, f32[512,768]{1,0:T(8,128)}), (f32[512,768]{1,0:T(8,128)}, f32[512,768]{1,0:T(8,128)})) %all-reduce.15.cloned.1.call-update) | async-done | bytes 3145744 | tf_op jit(solution)/shard_map/psum | solution.py:195
  820.6 4.1 fusion.26
  828.1 4.7 all-to-all-start
  837.8 89.3 %all-reduce.1 = (f32[3]{0:T(128)S(1)}, f32[768]{0:T(1024)}, f32[768]{0:T(1024)}, f32[3,384]{1,0:T(4,128)}, f32[768]{0:T(1024)}, /*index=5*/f32[768]{0:T(1024)}, f32[768]{0:T(1024)}, f32[1536]{0:T(1024)}, f32[768]{0:T(1024)}) all-reduce(f32[3]{0:T(128)S(1)} %pad_maximum_fusion.5, ...), channel_id=1, replica_groups=mesh['fsdp'=4,'context'=4,'tensor'=2] {'fsdp','context'}, use_global_device_ids=true, to_apply=%region_25.27 | all-reduce | flops 7299 | bytes 58392 | tf_op jit(solution)/shard_map/psum | solution.py:258
  932.4 38.8 %reduce-scatter.9.cloned.1.call-done = f32[48,1536]{1,0:T(8,128)} async-done(((f32[768,1536]{1,0:T(8,128)}), f32[48,1536]{1,0:T(8,128)}) %reduce-scatter.9.cloned.1.call-update) | async-done | bytes 294928 | tf_op jit(solution)/shard_map/reduce_scatter | solution.py:255
  971.2 79.1 %reduce-scatter.11.cloned.1.call-done = f32[1536,48]{0,1:T(8,128)} async-done(((f32[1536,768]{0,1:T(8,128)}), f32[1536,48]{0,1:T(8,128)}) %reduce-scatter.11.cloned.1.call-update) | async-done | bytes 294928 | tf_op jit(solution)/shard_map/reduce_scatter | solution.py:256
  1050.3 95.4 %all-reduce.13.cloned.1.call-done = (f32[6,64,64]{2,1,0:T(8,128)}, f32[6,64,64]{2,1,0:T(8,128)}) async-done(((f32[6,64,64]{2,1,0:T(8,128)}, f32[6,64,64]{2,1,0:T(8,128)}), (f32[6,64,64]{2,1,0:T(8,128)}, f32[6,64,64]{2,1,0:T(8,128)})) %all-reduce.13.cloned.1.call-update) | async-done | bytes 196624 | tf_op jit(solution)/shard_map/psum | solution.py:258
  1145.7 71.5 %reduce-scatter.5.cloned.1.call-done = f32[48,3,384]{2,0,1:T(8,128)} async-done(((f32[768,3,384]{2,0,1:T(8,128)}), f32[48,3,384]{2,0,1:T(8,128)}) %reduce-scatter.5.cloned.1.call-update) | async-done | bytes 221200 | tf_op jit(solution)/shard_map/reduce_scatter | solution.py:253
  (544 shorter events, 286.4 us)
Async XLA Ops:
  7.2 62.7 %copy-start = (f32[6,64,64]{2,1,0:T(8,128)S(1)}, f32[6,64,64]{2,1,0:T(8,128)}, u32[]{:S(2)}) copy-start(f32[6,64,64]{2,1,0:T(8,128)} %param.31) | copy-start | bytes 294916
  7.2 53.1 %all-gather.13.cloned.1.call-start = ((), (), s32[]{:S(2)}) async-start(), calls=%async_computation.6 | async-start | bytes 3760128 | tf_op jit(solution)/shard_map/all_gather | solution.py:154
  8.0 166.0 %all-gather.21.cloned.1.call-start = ((), (), s32[]{:S(2)}) async-start(), calls=%async_computation.16 | async-start | bytes 3342336 | tf_op jit(solution)/shard_map/all_gather | solution.py:13
  8.8 70.6 %copy-start.114 = (s32[4,1]{0,1:T(1,128)}, s32[4,1]{0,1:T(1,128)S(1)}, u32[]{:S(2)}) copy-start(s32[4,1]{0,1:T(1,128)S(1)} %reduce-window.4) | copy-start | bytes 52
  8.8 51.4 %copy-start.95 = (f32[768]{0:T(1024)S(1)}, f32[768]{0:T(1024)}, u32[]{:S(2)}) copy-start(f32[768]{0:T(1024)} %param.26) | copy-start | bytes 9220
  8.8 51.4 %copy-start.111 = (f32[768]{0:T(1024)S(1)}, f32[768]{0:T(1024)}, u32[]{:S(2)}) copy-start(f32[768]{0:T(1024)} %param.27) | copy-start | bytes 9220
  8.8 51.4 %copy-start.119 = (f32[3,384]{1,0:T(4,128)S(1)}, f32[3,384]{1,0:T(4,128)}, u32[]{:S(2)}) copy-start(f32[3,384]{1,0:T(4,128)} %param.29) | copy-start | bytes 13828
  10.5 67.7 %copy-start.79 = (s32[512]{0:T(512)}, s32[512]{0:T(512)S(1)}, u32[]{:S(2)}) copy-start(s32[512]{0:T(512)S(1)} %select_select_fusion) | copy-start | bytes 6148
  11.1 57.6 %copy-start.92 = (f32[512]{0:T(512)}, f32[512]{0:T(512)S(1)}, u32[]{:S(2)}) copy-start(f32[512]{0:T(512)S(1)} %broadcast_multiply_fusion.2) | copy-start | bytes 6148
  11.5 57.3 %copy-start.99 = (f32[512]{0:T(512)}, f32[512]{0:T(512)S(1)}, u32[]{:S(2)}) copy-start(f32[512]{0:T(512)S(1)} %fusion.133) | copy-start | bytes 6148
  13.2 150.8 %copy-start.75 = (f32[512]{0:T(512)}, f32[512]{0:T(512)S(1)}, u32[]{:S(2)}) copy-start(f32[512]{0:T(512)S(1)} %get-tuple-element.642) | copy-start | bytes 6148
  72.0 429.7 %copy-start.58 = (f32[512,6]{0,1:T(8,128)}, f32[512,6]{0,1:T(8,128)S(1)}, u32[]{:S(2)}) copy-start(f32[512,6]{0,1:T(8,128)S(1)} %get-tuple-element.645) | copy-start | bytes 36868
  74.1 51.5 %copy-start.24 = (f32[512,6,64]{0,2,1:T(8,128)}, f32[512,6,64]{0,2,1:T(8,128)S(1)}, u32[]{:S(2)}) copy-start(f32[512,6,64]{0,2,1:T(8,128)S(1)} %get-tuple-element.656) | copy-start | bytes 2359300
  74.1 51.5 %copy-start.26 = (f32[512,6,64]{0,2,1:T(8,128)}, f32[512,6,64]{0,2,1:T(8,128)S(1)}, u32[]{:S(2)}) copy-start(f32[512,6,64]{0,2,1:T(8,128)S(1)} %get-tuple-element.657) | copy-start | bytes 2359300
  76.8 220.4 %all-gather.15.cloned.1.call-start = ((), (), s32[]{:S(2)}) async-start(), calls=%async_computation.7 | async-start | bytes 1253376 | tf_op jit(solution)/shard_map/all_gather | solution.py:155
  77.6 271.8 %all-gather.19.cloned.1.call-start = ((), (), s32[]{:S(2)}) async-start(), calls=%async_computation.10 | async-start | bytes 5013504 | tf_op jit(solution)/shard_map/all_gather | solution.py:157
  78.1 282.6 %all-reduce.9.cloned.1.call-start = ((), (), s32[]{:S(2)}) async-start(), calls=%async_computation.8 | async-start | bytes 3145728 | tf_op jit(solution)/shard_map/psum | solution.py:181
  129.2 33.3 %copy-start.32 = (f32[512,6,64]{0,2,1:T(8,128)}, f32[512,6,64]{0,2,1:T(8,128)S(1)}, u32[]{:S(2)}) copy-start(f32[512,6,64]{0,2,1:T(8,128)S(1)} %get-tuple-element.650) | copy-start | bytes 2359300
  129.2 33.3 %copy-start.63 = (f32[512,6]{0,1:T(8,128)}, f32[512,6]{0,1:T(8,128)S(1)}, u32[]{:S(2)}) copy-start(f32[512,6]{0,1:T(8,128)S(1)} %get-tuple-element.649) | copy-start | bytes 36868
  130.5 32.0 %copy-start.34 = (f32[512,6,64]{0,2,1:T(8,128)}, f32[512,6,64]{0,2,1:T(8,128)S(1)}, u32[]{:S(2)}) copy-start(f32[512,6,64]{0,2,1:T(8,128)S(1)} %get-tuple-element.652) | copy-start | bytes 2359300
  130.5 32.0 %copy-start.66 = (f32[512,6]{0,1:T(8,128)}, f32[512,6]{0,1:T(8,128)S(1)}, u32[]{:S(2)}) copy-start(f32[512,6]{0,1:T(8,128)S(1)} %get-tuple-element.651) | copy-start | bytes 36868
  162.6 126.7 %copy-start.2 = (f32[512,6,64]{0,2,1:T(8,128)}, f32[512,6,64]{0,2,1:T(8,128)S(1)}, u32[]{:S(2)}) copy-start(f32[512,6,64]{0,2,1:T(8,128)S(1)} %get-tuple-element.658) | copy-start | bytes 2359300
  162.6 126.7 %copy-start.5 = (f32[512,6,64]{0,2,1:T(8,128)}, f32[512,6,64]{0,2,1:T(8,128)S(1)}, u32[]{:S(2)}) copy-start(f32[512,6,64]{0,2,1:T(8,128)S(1)} %get-tuple-element.659) | copy-start | bytes 2359300
  303.8 106.3 %all-gather.17.cloned.1.call-start = ((), (), s32[]{:S(2)}) async-start(), calls=%async_computation.9 | async-start | bytes 5013504 | tf_op jit(solution)/shard_map/all_gather | solution.py:156
  304.4 39.4 %all-to-all-start.1 = ((f32[8,64,768]{2,1,0:T(8,128)}), f32[8,64,768]{2,1,0:T(8,128)S(1)}, u32[]{:S(2)}, u32[]{:S(2)}) async-start(f32[8,64,768]{2,1,0:T(8,128)} %bitcast.190), calls=%async_computation.1 | async-start | bytes 3145728 | tf_op jit(solution)/shard_map/all_to_all | solution.py:203
  308.0 177.9 %all-reduce.11.cloned.1.call-start = ((), (), s32[]{:S(2)}) async-start(), calls=%async_computation.11 | async-start | bytes 3145728 | tf_op jit(solution)/shard_map/psum | solution.py:214
  309.3 180.0 %copy-start.97 = (f32[512]{0:T(512)}, f32[512]{0:T(512)S(1)}, u32[]{:S(2)}) copy-start(f32[512]{0:T(512)S(1)} %fusion.132) | copy-start | bytes 6148
  310.0 35.6 %copy-start.121 = (s32[8]{0:T(128)}, s32[8]{0:T(128)S(1)}, u32[]{:S(2)}) copy-start(s32[8]{0:T(128)S(1)} %get-tuple-element.629) | copy-start | bytes 100
  362.4 47.7 %copy-start.73 = (f32[768]{0:T(1024)S(1)}, f32[768]{0:T(1024)}, u32[]{:S(2)}) copy-start(f32[768]{0:T(1024)} %param.34) | copy-start | bytes 9220
  362.4 47.7 %copy-start.83 = (f32[768]{0:T(1024)S(1)}, f32[768]{0:T(1024)}, u32[]{:S(2)}) copy-start(f32[768]{0:T(1024)} %param.35) | copy-start | bytes 9220
  362.4 47.7 %copy-start.118 = (f32[1536]{0:T(1024)S(1)}, f32[1536]{0:T(1024)}, u32[]{:S(2)}) copy-start(f32[1536]{0:T(1024)} %param.37) | copy-start | bytes 18436
  362.5 126.2 %copy-start.81 = (f32[512]{0:T(512)}, f32[512]{0:T(512)S(1)}, u32[]{:S(2)}) copy-start(f32[512]{0:T(512)S(1)} %broadcast_multiply_fusion.1) | copy-start | bytes 6148
  362.8 125.9 %copy-start.90 = (f32[512]{0:T(512)}, f32[512]{0:T(512)S(1)}, u32[]{:S(2)}) copy-start(f32[512]{0:T(512)S(1)} %fusion.134) | copy-start | bytes 6148
  410.1 16.5 %copy-start.117 = (f32[768,1536]{1,0:T(8,128)S(1)}, f32[768,1536]{1,0:T(8,128)}, u32[]{:S(2)}) copy-start(f32[768,1536]{1,0:T(8,128)} %all-gather.17.cloned.1.call-done) | copy-start | bytes 14155780
  435.7 117.6 %all-gather.23.cloned.1.call-start = ((), (), s32[]{:S(2)}) async-start(), calls=%async_computation.17 | async-start | bytes 3342336 | tf_op jit(solution)/shard_map/all_gather | solution.py:13
  497.9 322.7 %all-reduce.15.cloned.1.call-start = ((), (), s32[]{:S(2)}) async-start(), calls=%async_computation.19 | async-start | bytes 6291456 | tf_op jit(solution)/shard_map/psum | solution.py:195
  503.5 12.7 %copy-start.7 = (f32[512,6,64]{0,2,1:T(8,128)S(1)}, f32[512,6,64]{0,2,1:T(8,128)}, u32[]{:S(2)}) copy-start(f32[512,6,64]{0,2,1:T(8,128)} %copy-done.5) | copy-start | bytes 2359300
  737.9 194.5 %reduce-scatter.7.cloned.1.call-start = ((), (), s32[]{:S(2)}) async-start(), calls=%async_computation.13 | async-start | bytes 1253376 | tf_op jit(solution)/shard_map/reduce_scatter | solution.py:254
  743.4 227.8 %reduce-scatter.9.cloned.1.call-start = ((), (), s32[]{:S(2)}) async-start(), calls=%async_computation.14 | async-start | bytes 5013504 | tf_op jit(solution)/shard_map/reduce_scatter | solution.py:255
  755.6 294.7 %reduce-scatter.11.cloned.1.call-start = ((), (), s32[]{:S(2)}) async-start(), calls=%async_computation.15 | async-start | bytes 5013504 | tf_op jit(solution)/shard_map/reduce_scatter | solution.py:256
  767.8 377.9 %all-reduce.13.cloned.1.call-start = ((), (), s32[]{:S(2)}) async-start(), calls=%async_computation.18 | async-start | bytes 786432 | tf_op jit(solution)/shard_map/psum | solution.py:258
  772.4 444.8 %reduce-scatter.5.cloned.1.call-start = ((), (), s32[]{:S(2)}) async-start(), calls=%async_computation.12 | async-start | bytes 3760128 | tf_op jit(solution)/shard_map/reduce_scatter | solution.py:253
  782.8 37.8 %copy-start.98 = (f32[512]{0:T(512)S(1)}, f32[512]{0:T(512)}, u32[]{:S(2)}) copy-start(f32[512]{0:T(512)} %copy-done.97) | copy-start | bytes 6148
  782.8 37.8 %copy-start.104 = (f32[768]{0:T(1024)S(1)}, f32[768]{0:T(1024)}, u32[]{:S(2)}) copy-start(f32[768]{0:T(1024)} %param.33) | copy-start | bytes 9220
  782.8 37.8 %copy-start.113 = (f32[768]{0:T(1024)S(1)}, f32[768]{0:T(1024)}, u32[]{:S(2)}) copy-start(f32[768]{0:T(1024)} %param.39) | copy-start | bytes 9220
  828.1 102.2 %all-to-all-start = ((f32[8,64,768]{2,1,0:T(8,128)}), f32[8,64,768]{2,1,0:T(8,128)}, u32[]{:S(2)}, u32[]{:S(2)}) async-start(f32[8,64,768]{2,1,0:T(8,128)} %broadcast_select_fusion.1), calls=%async_computation | async-start | bytes 3145728 | tf_op jit(solution)/shard_map/all_to_all | solution.py:198
  837.0 90.5 %copy-start.102 = (f32[512]{0:T(512)S(1)}, f32[512]{0:T(512)}, u32[]{:S(2)}) copy-start(f32[512]{0:T(512)} %copy-done.101) | copy-start | bytes 6148
  837.0 90.5 %copy-start.49 = (f32[512,768]{1,0:T(8,128)S(1)}, f32[512,768]{1,0:T(8,128)}, u32[]{:S(2)}) copy-start(f32[512,768]{1,0:T(8,128)} %get-tuple-element.616) | copy-start | bytes 4718596
  (93 other events, 293.9 us)
Sparse Core Ops, SparseCore 0:
  10.4 49.8 all-gather.12
  76.9 44.2 all-gather.20
  123.5 36.9 all-gather.14
  162.7 51.7 all-gather.18
  304.0 50.9 all-reduce.8
  357.1 52.9 all-gather.16
  435.8 50.0 all-reduce.10
  498.0 45.7 all-gather.22
  738.0 82.5 all-reduce.14
  824.7 67.4 reduce-scatter.6
  896.6 74.5 reduce-scatter.8
  975.5 74.7 reduce-scatter.10
  1054.9 90.7 all-reduce.12
  1150.0 67.1 reduce-scatter.4
where the time goes:
time: 1240 us; the launch traced here: 1230 us
  waiting for transfers between devices  503 us (41%)
  blocking collectives  200 us (16%)
  matrix products  192 us (15%)
  other arithmetic  149 us (12%)
  local copies, waits for them, and re-layouts  136 us (11%)
  loops' own time  21.4 us (2%)
  between operations  17.7 us (1%)
    select_n x64, other arithmetic, lap(): return jax.tree.map(lambda a, b: jnp.where(reached, a, b), new, before)  103 us
    dynamic_slice x96, local copies, waits for them, and re-layouts, lap(): new = combine(before, jax.tree.map(lambda part: part[at], everything))  99.5 us
    psum x1, waiting for transfers between devices, body(): lax.psum((grad_ln1_gain, grad_ln1_shift, grad_qkv_bias, grad_feat_query,...  95.4 us
    psum x1, blocking collectives, body(): lax.psum((grad_ln1_gain, grad_ln1_shift, grad_qkv_bias, grad_feat_query,...  89.3 us
    reduce_scatter x1, waiting for transfers between devices, body(): lax.psum_scatter(grad_down_full, ('fsdp', 'context'), scatter_dimension=1...  79.1 us
    reduce_scatter x1, waiting for transfers between devices, body(): lax.psum_scatter(grad_qkv_full, ('fsdp', 'context'), scatter_dimension=0,...  71.5 us
    all_gather x2, blocking collectives, entering(): everything = jax.tree.map(lambda part: lax.all_gather(part, axis), x)  67.3 us
    psum x1, waiting for transfers between devices, body(): grad_normed2 = lax.psum(grad_normed2_part, 'tensor')  50 us
  transfers between devices with their start and end apart: 16, of which 9 were waited for; matrix products, arithmetic and copies ran while one was open for 20% of the time, Pallas kernels for 0%

commit v1 on v0

--- a/solution.py
+++ b/solution.py
@@ -6,6 +6,28 @@
 
 HIGH = lax.Precision.HIGHEST
 NORM_EPS = 1e-05
+
+
+def split_up(x, dim, size):
+    before, after = (x.shape[:dim], x.shape[dim + 1 :])
+    return jnp.moveaxis(x.reshape(*before, size, -1, *after), dim, 0)
+
+
+def in_order(pieces, dim):
+    dims = list(pieces.shape[1:])
+    dims[dim] *= pieces.shape[0]
+    return jnp.moveaxis(pieces, 0, dim).reshape(dims)
+
+
+def exchange_in_pairs(shard, axis, split_dim, concat_dim):
+    length, here = (lax.axis_size(axis), lax.axis_index(axis))
+    blocks = split_up(shard, split_dim, length)
+    finished = [blocks[here]]
+    for step in range(1, length):
+        sent = blocks[here ^ step]
+        finished.append(lax.ppermute(sent, axis, [(i, i ^ step) for i in range(length)]))
+    blocks = jnp.stack(finished)[here ^ jnp.arange(length)]
+    return in_order(blocks, concat_dim)
 
 
 def entering(x, axis, combine, identity, reverse):
@@ -200,13 +222,7 @@
     squares = jnp.stack(
         [jnp.sum(valid * result * result), jnp.sum(valid * attn * attn), jnp.sum(valid * mlp * mlp)]
     )
-    inbound = lax.all_to_all(
-        cotangent.reshape(slots, group_rows, width),
-        "context",
-        split_axis=0,
-        concat_axis=0,
-        tiled=True,
-    )
+    inbound = exchange_in_pairs(cotangent.reshape(slots, group_rows, width), "context", 0, 0)
     grad_y = jnp.take(inbound, slot_of, axis=0).reshape(count_rows, width) * valid
     grad_down_bias = jnp.sum(grad_y, axis=0)
     _, mlp_backward = jax.vjp(mlp_part, normed2, up_full, up_bias, down_full)

time: 1240 us -> 1240 us (level)
    all_to_all x1 -> x0, waiting for transfers between devices: 33.8 us -> none  [body(): lax.all_to_all(cotangent.reshape(slots, group_rows, width), 'context', sp...]
    ppermute x0 -> x3, waiting for transfers between devices: none -> 27.5 us  [exchange_in_pairs(): lax.ppermute(sent, axis, [(i, i ^ step) for i in range(length)])]
  transfers between devices with their start and end apart: 16 -> 18, of which waited for: 9 -> 10; matrix products, arithmetic and copies ran while one was open for 20% -> 20% of each run, Pallas kernels for 0% -> 0%
where the time goes in v1:
time: 1240 us; the launch traced here: 1230 us
  waiting for transfers between devices  500 us (40%)
  blocking collectives  199 us (16%)
  matrix products  192 us (15%)
  other arithmetic  148 us (12%)
  local copies, waits for them, and re-layouts  139 us (11%)
  loops' own time  21.4 us (2%)
  between operations  17.8 us (1%)
    select_n x64, other arithmetic, lap(): return jax.tree.map(lambda a, b: jnp.where(reached, a, b), new, before)  103 us
    dynamic_slice x96, local copies, waits for them, and re-layouts, lap(): new = combine(before, jax.tree.map(lambda part: part[at], everything))  100 us
    psum x1, waiting for transfers between devices, body(): lax.psum((grad_ln1_gain, grad_ln1_shift, grad_qkv_bias, grad_feat_query,...  95.4 us
    psum x1, blocking collectives, body(): lax.psum((grad_ln1_gain, grad_ln1_shift, grad_qkv_bias, grad_feat_query,...  89.2 us
    reduce_scatter x1, waiting for transfers between devices, body(): lax.psum_scatter(grad_down_full, ('fsdp', 'context'), scatter_dimension=1...  79.1 us
    reduce_scatter x1, waiting for transfers between devices, body(): lax.psum_scatter(grad_qkv_full, ('fsdp', 'context'), scatter_dimension=0,...  71.5 us
    all_gather x2, blocking collectives, entering(): everything = jax.tree.map(lambda part: lax.all_gather(part, axis), x)  67.3 us
    all_gather x1, waiting for transfers between devices, body(): lax.all_gather(up_weight, ('fsdp', 'context'), axis=0, tiled=True)  51 us
  transfers between devices with their start and end apart: 18, of which 10 were waited for; matrix products, arithmetic and copies ran while one was open for 20% of the time, Pallas kernels for 0%

profile of v1, /device:TPU:0, one launch (start us, length us, event | category | flops | bytes accessed | tf_op | source)
XLA Modules:
  0.0 1227.6 jit_solution(2083504591726448617)
XLA Ops:
  13.3 47.0 %all-gather.13.cloned.1.call-done = f32[768,3,384]{2,0,1:T(8,128)} async-done(((f32[48,3,384]{2,0,1:T(8,128)}), f32[768,3,384]{2,0,1:T(8,128)}) %all-gather.13.cloned.1.call-update) | async-done | bytes 3538960 | tf_op jit(solution)/shard_map/all_gather | solution.py:176
  60.3 8.5 convolution_add_fusion.1
  74.2 2.6 fusion.35
  82.3 42.9 %all-reduce = f32[16]{0:T(128)} all-reduce(f32[16]{0:T(128)S(1)} %dynamic-update-slice), channel_id=1, replica_groups=mesh['fsdp'=4,'context'=4,'tensor'=2] {'fsdp','context'}, use_global_device_ids=true, to_apply=%add | all-reduce | flops 16 | bytes 128
  130.1 31.8 %all-gather.4 = f32[16,6,128]{2,1,0:T(8,128)} all-gather(f32[1,6,128]{2,1,0:T(8,128)S(1)} %bitcast.212), channel_id=3, replica_groups=mesh['fsdp'=4,'context'=4,'tensor'=2] {'fsdp','context'}, dimensions={0}, use_global_device_ids=true | all-gather | bytes 52224 | tf_op jit(solution)/shard_map/all_gather | solution.py:35
  165.5 8.0 multiply_reduce_fusion
  173.5 112.2 %while.22 = (s32[]{:T(128)}, f32[6,128,64]{2,1,0:T(8,128)}, f32[6,128]{1,0:T(8,128)}, s32[]{:T(128)}, f32[16,6,128,64]{2,3,1,0:T(8,128)}, /*index=5*/f32[16]{0:T...) while((s32[]{:T(128)}, f32[6,128,64]{2,1,0:T(8,128)}, f32[6,128]{1,0:T(8,128)}, ...), condition=%wide.region_15.16_spmd.clone, body=%wide.region_14.15_spmd.clone.sunk | while | flops 199685 | bytes 1385643 | solution.py:46
  291.0 6.3 fusion.59
  297.3 6.5 fusion.168
  311.8 7.5 collective-permute-done.2
  319.3 20.0 %collective-permute-done.1 = f32[2,64,768]{2,1,0:T(8,128)S(1)} collective-permute-done((f32[2,64,768]{2,1,0:T(8,128)S(1)}, f32[2,64,768]{2,1,0:T(8,128)S(1)}, u32[]{:S(2)}, u32[]{:S(2)}) %collective-permute-start.1) | collective-permute-done | bytes 393248 | tf_op jit(solution)/shard_map/ppermute | solution.py:28
  345.6 11.4 fusion.169
  359.1 51.0 %all-gather.17.cloned.1.call-done = f32[768,1536]{1,0:T(8,128)} async-done(((f32[48,1536]{1,0:T(8,128)}), f32[768,1536]{1,0:T(8,128)}) %all-gather.17.cloned.1.call-update) | async-done | bytes 4718608 | tf_op jit(solution)/shard_map/all_gather | solution.py:178
  410.1 14.9 %fusion.156 = (f32[1536]{0:T(1024)}, f32[512,1536]{1,0:T(8,128)S(1)}, f32[512,1536]{1,0:T(8,128)}) fusion(f32[512,1536]{1,0:T(8,128)} %fusion.169, f32[1536]{0:T(1024)S(1)} %copy-done.119, f32[768,1536]{1,0:T(8,128)} %all-gather.17.cloned.1.call-done, f32[512,768]{1,0:T(8,128)S(1)} %get-tuple-element.631, f32[768]{0:T(1024)S(1)} %copy-done.84, ...), kind=kOutput, calls=%fused_computation.266 | convolution fusion | flops 7265843712 | bytes 15751168 | tf_op jit(solution)/shard_map/dot_general | solution.py:74
  426.6 9.1 fusion.170
  435.9 50.0 %all-reduce.11.cloned.1.call-done = f32[512,768]{1,0:T(8,128)} async-done(((f32[512,768]{1,0:T(8,128)}), f32[512,768]{1,0:T(8,128)}) %all-reduce.11.cloned.1.call-update) | async-done | bytes 1572880 | tf_op jit(solution)/shard_map/psum | solution.py:230
  485.9 2.7 multiply_reduce_fusion.2
  495.3 2.6 fusion.71
  498.8 2.9 pad_maximum_fusion.1
  503.5 12.7 %fusion.38 = f32[512,768]{1,0:T(8,128)} fusion(f32[1536,768]{0,1:T(8,128)} %all-gather.19.cloned.1.call-done, f32[512,1536]{1,0:T(8,128)S(1)} %copy-done.125), kind=kOutput, calls=%fused_computation.82 | convolution fusion | flops 7254048768 | bytes 9437184 | tf_op jit(solution)/shard_map/dot_general | solution.py:75
  517.7 35.5 %all-gather.5 = f32[16,6,128]{2,1,0:T(8,128)} all-gather(f32[1,6,128]{2,1,0:T(8,128)S(1)} %fusion.126), channel_id=5, replica_groups=mesh['fsdp'=4,'context'=4,'tensor'=2] {'fsdp','context'}, dimensions={0}, use_global_device_ids=true | all-gather | bytes 52224 | tf_op jit(solution)/shard_map/all_gather | solution.py:35
  553.3 112.1 %while.23 = (s32[]{:T(128)}, f32[6,128,64]{2,1,0:T(8,128)}, f32[6,128]{1,0:T(8,128)}, s32[]{:T(128)}, f32[16,6,128,64]{2,3,1,0:T(8,128)}, /*index=5*/f32[16]{0:T...) while((s32[]{:T(128)}, f32[6,128,64]{2,1,0:T(8,128)}, ...), condition=%wide.region_31.33_spmd.clone, body=%wide.region_30.32_spmd.clone.sunk | while | flops 199689 | bytes 1385705 | solution.py:46
  666.6 2.2 and_convert_fusion
  668.8 2.6 copy.110
  671.4 7.3 fusion.172
  678.8 5.1 fusion.88
  684.0 5.4 fusion.12
  689.3 8.5 fusion.13
  697.9 4.1 fusion.8
  705.3 2.3 copy.118
  707.6 3.3 bitcast_add_fusion.4
  714.7 2.3 copy.117
  717.1 2.7 fusion.90
  725.7 2.3 copy.116
  728.0 10.4 convolution_bitcast_fusion
  738.5 5.4 fusion.173
  744.0 12.1 fusion.62
  756.2 12.1 fusion.37
  768.4 3.0 fusion.83
  773.2 10.1 fusion.30
  784.2 37.0 %all-reduce.15.cloned.1.call-done = (f32[512,768]{1,0:T(8,128)}, f32[512,768]{1,0:T(8,128)}) async-done(((f32[512,768]{1,0:T(8,128)}, f32[512,768]{1,0:T(8,128)}), (f32[512,768]{1,0:T(8,128)}, f32[512,768]{1,0:T(8,128)})) %all-reduce.15.cloned.1.call-update) | async-done | bytes 3145744 | tf_op jit(solution)/shard_map/psum | solution.py:217
  821.1 4.1 fusion.26
  828.6 4.7 all-to-all-start
  838.3 89.2 %all-reduce.1 = (f32[3]{0:T(128)S(1)}, f32[768]{0:T(1024)}, f32[768]{0:T(1024)}, f32[3,384]{1,0:T(4,128)}, f32[768]{0:T(1024)}, /*index=5*/f32[768]{0:T(1024)}, f32[768]{0:T(1024)}, f32[1536]{0:T(1024)}, f32[768]{0:T(1024)}) all-reduce(f32[3]{0:T(128)S(1)} %pad_maximum_fusion.6, ...), channel_id=1, replica_groups=mesh['fsdp'=4,'context'=4,'tensor'=2] {'fsdp','context'}, use_global_device_ids=true, to_apply=%region_25.27 | all-reduce | flops 7299 | bytes 58392 | tf_op jit(solution)/shard_map/psum | solution.py:274
  932.9 38.8 %reduce-scatter.9.cloned.1.call-done = f32[48,1536]{1,0:T(8,128)} async-done(((f32[768,1536]{1,0:T(8,128)}), f32[48,1536]{1,0:T(8,128)}) %reduce-scatter.9.cloned.1.call-update) | async-done | bytes 294928 | tf_op jit(solution)/shard_map/reduce_scatter | solution.py:271
  971.7 79.1 %reduce-scatter.11.cloned.1.call-done = f32[1536,48]{0,1:T(8,128)} async-done(((f32[1536,768]{0,1:T(8,128)}), f32[1536,48]{0,1:T(8,128)}) %reduce-scatter.11.cloned.1.call-update) | async-done | bytes 294928 | tf_op jit(solution)/shard_map/reduce_scatter | solution.py:272
  1050.8 95.4 %all-reduce.13.cloned.1.call-done = (f32[6,64,64]{2,1,0:T(8,128)}, f32[6,64,64]{2,1,0:T(8,128)}) async-done(((f32[6,64,64]{2,1,0:T(8,128)}, f32[6,64,64]{2,1,0:T(8,128)}), (f32[6,64,64]{2,1,0:T(8,128)}, f32[6,64,64]{2,1,0:T(8,128)})) %all-reduce.13.cloned.1.call-update) | async-done | bytes 196624 | tf_op jit(solution)/shard_map/psum | solution.py:274
  1146.2 71.5 %reduce-scatter.5.cloned.1.call-done = f32[48,3,384]{2,0,1:T(8,128)} async-done(((f32[768,3,384]{2,0,1:T(8,128)}), f32[48,3,384]{2,0,1:T(8,128)}) %reduce-scatter.5.cloned.1.call-update) | async-done | bytes 221200 | tf_op jit(solution)/shard_map/reduce_scatter | solution.py:269
  (555 shorter events, 293.4 us)
Async XLA Ops:
  7.2 62.7 %copy-start = (f32[6,64,64]{2,1,0:T(8,128)S(1)}, f32[6,64,64]{2,1,0:T(8,128)}, u32[]{:S(2)}) copy-start(f32[6,64,64]{2,1,0:T(8,128)} %param.31) | copy-start | bytes 294916
  7.2 53.1 %all-gather.13.cloned.1.call-start = ((), (), s32[]{:S(2)}) async-start(), calls=%async_computation.5 | async-start | bytes 3760128 | tf_op jit(solution)/shard_map/all_gather | solution.py:176
  8.0 165.6 %all-gather.21.cloned.1.call-start = ((), (), s32[]{:S(2)}) async-start(), calls=%async_computation.15 | async-start | bytes 3342336 | tf_op jit(solution)/shard_map/all_gather | solution.py:35
  8.8 70.6 %copy-start.115 = (s32[4,1]{0,1:T(1,128)}, s32[4,1]{0,1:T(1,128)S(1)}, u32[]{:S(2)}) copy-start(s32[4,1]{0,1:T(1,128)S(1)} %reduce-window.4) | copy-start | bytes 52
  8.8 51.4 %copy-start.96 = (f32[768]{0:T(1024)S(1)}, f32[768]{0:T(1024)}, u32[]{:S(2)}) copy-start(f32[768]{0:T(1024)} %param.26) | copy-start | bytes 9220
  8.8 51.4 %copy-start.112 = (f32[768]{0:T(1024)S(1)}, f32[768]{0:T(1024)}, u32[]{:S(2)}) copy-start(f32[768]{0:T(1024)} %param.27) | copy-start | bytes 9220
  8.8 51.4 %copy-start.120 = (f32[3,384]{1,0:T(4,128)S(1)}, f32[3,384]{1,0:T(4,128)}, u32[]{:S(2)}) copy-start(f32[3,384]{1,0:T(4,128)} %param.29) | copy-start | bytes 13828
  10.5 67.7 %copy-start.80 = (s32[512]{0:T(512)}, s32[512]{0:T(512)S(1)}, u32[]{:S(2)}) copy-start(s32[512]{0:T(512)S(1)} %select_select_fusion) | copy-start | bytes 6148
  11.1 57.6 %copy-start.93 = (f32[512]{0:T(512)}, f32[512]{0:T(512)S(1)}, u32[]{:S(2)}) copy-start(f32[512]{0:T(512)S(1)} %broadcast_multiply_fusion.2) | copy-start | bytes 6148
  11.5 57.3 %copy-start.100 = (f32[512]{0:T(512)}, f32[512]{0:T(512)S(1)}, u32[]{:S(2)}) copy-start(f32[512]{0:T(512)S(1)} %fusion.133) | copy-start | bytes 6148
  13.3 150.3 %copy-start.76 = (f32[512]{0:T(512)}, f32[512]{0:T(512)S(1)}, u32[]{:S(2)}) copy-start(f32[512]{0:T(512)S(1)} %get-tuple-element.646) | copy-start | bytes 6148
  72.0 429.7 %copy-start.59 = (f32[512,6]{0,1:T(8,128)}, f32[512,6]{0,1:T(8,128)S(1)}, u32[]{:S(2)}) copy-start(f32[512,6]{0,1:T(8,128)S(1)} %get-tuple-element.649) | copy-start | bytes 36868
  74.1 51.1 %copy-start.24 = (f32[512,6,64]{0,2,1:T(8,128)}, f32[512,6,64]{0,2,1:T(8,128)S(1)}, u32[]{:S(2)}) copy-start(f32[512,6,64]{0,2,1:T(8,128)S(1)} %get-tuple-element.660) | copy-start | bytes 2359300
  74.1 51.1 %copy-start.26 = (f32[512,6,64]{0,2,1:T(8,128)}, f32[512,6,64]{0,2,1:T(8,128)S(1)}, u32[]{:S(2)}) copy-start(f32[512,6,64]{0,2,1:T(8,128)S(1)} %get-tuple-element.661) | copy-start | bytes 2359300
  76.8 220.4 %all-gather.15.cloned.1.call-start = ((), (), s32[]{:S(2)}) async-start(), calls=%async_computation.6 | async-start | bytes 1253376 | tf_op jit(solution)/shard_map/all_gather | solution.py:177
  77.6 268.0 %all-gather.19.cloned.1.call-start = ((), (), s32[]{:S(2)}) async-start(), calls=%async_computation.9 | async-start | bytes 5013504 | tf_op jit(solution)/shard_map/all_gather | solution.py:179
  78.1 278.9 %all-reduce.9.cloned.1.call-start = ((), (), s32[]{:S(2)}) async-start(), calls=%async_computation.7 | async-start | bytes 3145728 | tf_op jit(solution)/shard_map/psum | solution.py:203
  128.8 33.3 %copy-start.32 = (f32[512,6,64]{0,2,1:T(8,128)}, f32[512,6,64]{0,2,1:T(8,128)S(1)}, u32[]{:S(2)}) copy-start(f32[512,6,64]{0,2,1:T(8,128)S(1)} %get-tuple-element.654) | copy-start | bytes 2359300
  128.8 33.3 %copy-start.64 = (f32[512,6]{0,1:T(8,128)}, f32[512,6]{0,1:T(8,128)S(1)}, u32[]{:S(2)}) copy-start(f32[512,6]{0,1:T(8,128)S(1)} %get-tuple-element.653) | copy-start | bytes 36868
  130.1 32.0 %copy-start.34 = (f32[512,6,64]{0,2,1:T(8,128)}, f32[512,6,64]{0,2,1:T(8,128)S(1)}, u32[]{:S(2)}) copy-start(f32[512,6,64]{0,2,1:T(8,128)S(1)} %get-tuple-element.656) | copy-start | bytes 2359300
  130.1 32.0 %copy-start.67 = (f32[512,6]{0,1:T(8,128)}, f32[512,6]{0,1:T(8,128)S(1)}, u32[]{:S(2)}) copy-start(f32[512,6]{0,1:T(8,128)S(1)} %get-tuple-element.655) | copy-start | bytes 36868
  162.1 127.2 %copy-start.2 = (f32[512,6,64]{0,2,1:T(8,128)}, f32[512,6,64]{0,2,1:T(8,128)S(1)}, u32[]{:S(2)}) copy-start(f32[512,6,64]{0,2,1:T(8,128)S(1)} %get-tuple-element.662) | copy-start | bytes 2359300
  162.1 127.2 %copy-start.5 = (f32[512,6,64]{0,2,1:T(8,128)}, f32[512,6,64]{0,2,1:T(8,128)S(1)}, u32[]{:S(2)}) copy-start(f32[512,6,64]{0,2,1:T(8,128)S(1)} %get-tuple-element.663) | copy-start | bytes 2359300
  303.9 106.2 %all-gather.17.cloned.1.call-start = ((), (), s32[]{:S(2)}) async-start(), calls=%async_computation.8 | async-start | bytes 5013504 | tf_op jit(solution)/shard_map/all_gather | solution.py:178
  304.4 181.5 %all-reduce.11.cloned.1.call-start = ((), (), s32[]{:S(2)}) async-start(), calls=%async_computation.10 | async-start | bytes 3145728 | tf_op jit(solution)/shard_map/psum | solution.py:230
  305.4 13.9 %collective-permute-start.2 = (f32[2,64,768]{2,1,0:T(8,128)S(1)}, f32[2,64,768]{2,1,0:T(8,128)S(1)}, u32[]{:S(2)}, u32[]{:S(2)}) collective-permute-start(f32[2,64,768]{2,1,0:T(8,128)S(1)} %get-tuple-element.636), channel_id=1, source_target_pairs={{0,6},{2,4},{4,2},{6,0},{1,7},{3,5},{5,3},{7,1},{8,14},{10,12},{12... | collective-permute-start | bytes 1179656 | tf_op jit(solution)/shard_map/ppermute | solution.py:28
  306.4 32.9 %collective-permute-start.1 = (f32[2,64,768]{2,1,0:T(8,128)S(1)}, f32[2,64,768]{2,1,0:T(8,128)S(1)}, u32[]{:S(2)}, u32[]{:S(2)}) collective-permute-start(f32[2,64,768]{2,1,0:T(8,128)S(1)} %get-tuple-element.637), channel_id=1, source_target_pairs={{0,4},{2,6},{4,0},{6,2},{1,5},{3,7},{5,1},{7,3},{8,12},{10,14},{12... | collective-permute-start | bytes 1179656 | tf_op jit(solution)/shard_map/ppermute | solution.py:28
  308.6 30.7 %collective-permute-start = (f32[2,64,768]{2,1,0:T(8,128)S(1)}, f32[2,64,768]{2,1,0:T(8,128)S(1)}, u32[]{:S(2)}, u32[]{:S(2)}) collective-permute-start(f32[2,64,768]{2,1,0:T(8,128)S(1)} %get-tuple-element.638), channel_id=1, source_target_pairs={{0,2},{2,0},{4,6},{6,4},{1,3},{3,1},{5,7},{7,5},{8,10},{10,8},{12,... | collective-permute-start | bytes 1179656 | tf_op jit(solution)/shard_map/ppermute | solution.py:28
  311.8 177.6 %copy-start.98 = (f32[512]{0:T(512)}, f32[512]{0:T(512)S(1)}, u32[]{:S(2)}) copy-start(f32[512]{0:T(512)S(1)} %fusion.132) | copy-start | bytes 6148
  358.7 51.4 %copy-start.74 = (f32[768]{0:T(1024)S(1)}, f32[768]{0:T(1024)}, u32[]{:S(2)}) copy-start(f32[768]{0:T(1024)} %param.34) | copy-start | bytes 9220
  358.7 51.4 %copy-start.84 = (f32[768]{0:T(1024)S(1)}, f32[768]{0:T(1024)}, u32[]{:S(2)}) copy-start(f32[768]{0:T(1024)} %param.35) | copy-start | bytes 9220
  358.7 51.4 %copy-start.119 = (f32[1536]{0:T(1024)S(1)}, f32[1536]{0:T(1024)}, u32[]{:S(2)}) copy-start(f32[1536]{0:T(1024)} %param.37) | copy-start | bytes 18436
  358.7 129.9 %copy-start.82 = (f32[512]{0:T(512)}, f32[512]{0:T(512)S(1)}, u32[]{:S(2)}) copy-start(f32[512]{0:T(512)S(1)} %broadcast_multiply_fusion.1) | copy-start | bytes 6148
  359.1 129.6 %copy-start.91 = (f32[512]{0:T(512)}, f32[512]{0:T(512)S(1)}, u32[]{:S(2)}) copy-start(f32[512]{0:T(512)S(1)} %fusion.134) | copy-start | bytes 6148
  410.1 16.5 %copy-start.118 = (f32[768,1536]{1,0:T(8,128)S(1)}, f32[768,1536]{1,0:T(8,128)}, u32[]{:S(2)}) copy-start(f32[768,1536]{1,0:T(8,128)} %all-gather.17.cloned.1.call-done) | copy-start | bytes 14155780
  435.7 117.6 %all-gather.23.cloned.1.call-start = ((), (), s32[]{:S(2)}) async-start(), calls=%async_computation.16 | async-start | bytes 3342336 | tf_op jit(solution)/shard_map/all_gather | solution.py:35
  497.9 323.2 %all-reduce.15.cloned.1.call-start = ((), (), s32[]{:S(2)}) async-start(), calls=%async_computation.18 | async-start | bytes 6291456 | tf_op jit(solution)/shard_map/psum | solution.py:217
  738.5 194.4 %reduce-scatter.7.cloned.1.call-start = ((), (), s32[]{:S(2)}) async-start(), calls=%async_computation.12 | async-start | bytes 1253376 | tf_op jit(solution)/shard_map/reduce_scatter | solution.py:270
  743.9 227.8 %reduce-scatter.9.cloned.1.call-start = ((), (), s32[]{:S(2)}) async-start(), calls=%async_computation.13 | async-start | bytes 5013504 | tf_op jit(solution)/shard_map/reduce_scatter | solution.py:271
  756.1 294.7 %reduce-scatter.11.cloned.1.call-start = ((), (), s32[]{:S(2)}) async-start(), calls=%async_computation.14 | async-start | bytes 5013504 | tf_op jit(solution)/shard_map/reduce_scatter | solution.py:272
  768.3 377.9 %all-reduce.13.cloned.1.call-start = ((), (), s32[]{:S(2)}) async-start(), calls=%async_computation.17 | async-start | bytes 786432 | tf_op jit(solution)/shard_map/psum | solution.py:274
  773.0 444.7 %reduce-scatter.5.cloned.1.call-start = ((), (), s32[]{:S(2)}) async-start(), calls=%async_computation.11 | async-start | bytes 3760128 | tf_op jit(solution)/shard_map/reduce_scatter | solution.py:269
  783.3 37.8 %copy-start.99 = (f32[512]{0:T(512)S(1)}, f32[512]{0:T(512)}, u32[]{:S(2)}) copy-start(f32[512]{0:T(512)} %copy-done.98) | copy-start | bytes 6148
  783.3 37.8 %copy-start.105 = (f32[768]{0:T(1024)S(1)}, f32[768]{0:T(1024)}, u32[]{:S(2)}) copy-start(f32[768]{0:T(1024)} %param.33) | copy-start | bytes 9220
  783.3 37.8 %copy-start.114 = (f32[768]{0:T(1024)S(1)}, f32[768]{0:T(1024)}, u32[]{:S(2)}) copy-start(f32[768]{0:T(1024)} %param.39) | copy-start | bytes 9220
  828.6 102.2 %all-to-all-start = ((f32[8,64,768]{2,1,0:T(8,128)}), f32[8,64,768]{2,1,0:T(8,128)}, u32[]{:S(2)}, u32[]{:S(2)}) async-start(f32[8,64,768]{2,1,0:T(8,128)} %broadcast_select_fusion.1), calls=%async_computation | async-start | bytes 3145728 | tf_op jit(solution)/shard_map/all_to_all | solution.py:220
  837.5 90.5 %copy-start.103 = (f32[512]{0:T(512)S(1)}, f32[512]{0:T(512)}, u32[]{:S(2)}) copy-start(f32[512]{0:T(512)} %copy-done.102) | copy-start | bytes 6148
  837.5 90.5 %copy-start.49 = (f32[512,768]{1,0:T(8,128)S(1)}, f32[512,768]{1,0:T(8,128)}, u32[]{:S(2)}) copy-start(f32[512,768]{1,0:T(8,128)} %get-tuple-element.616) | copy-start | bytes 4718596
  (96 other events, 310.1 us)
Sparse Core Ops, SparseCore 0:
  10.4 49.8 all-gather.12
  77.0 44.1 all-gather.20
  123.5 36.9 all-gather.14
  162.6 51.8 all-gather.18
  304.0 50.9 all-reduce.8
  357.1 52.9 all-gather.16
  435.8 50.0 all-reduce.10
  498.0 45.6 all-gather.22
  738.5 82.5 all-reduce.14
  825.2 67.4 reduce-scatter.6
  897.1 74.5 reduce-scatter.8
  976.0 74.7 reduce-scatter.10
  1055.4 90.7 all-reduce.12
  1150.5 67.1 reduce-scatter.4
